TPU v7x, 32 devices: a whole 2x2x4 slice. The times are simulated.
32 devices in a mesh: dp: 8 (over y, x, core), shard: 4 (over z).
Axes of the slice: x: 2, y: 2, z: 4, core: 2. Of those that a mesh axis runs over, the one named last changes fastest.
Arguments:
- activations: bfloat16 [4096, 4096], P('dp', 'shard'), may hold values from -6 to 6
- out_grads: bfloat16 [4096, 14336], P('dp', 'shard'), may hold values from -6 to 6
- sign_bits: int32 [14336], P('shard'), may hold values from 0 to 1
- block_ids: int32 [4, 8], replicated, may hold values from 0 to 111, as said below
Outputs:
- gram: float32 [4096, 1024], P('shard')
Inputs may be any that keep to these rules, and one draw needn't show every extreme that they name: `block_ids`: row o holds 4 runs of 2 entries; the entries of a run are distinct blocks of one shard s (ids s * 28 + 0 to s * 28 + 27), and the runs of a row come from distinct shards.
All inputs are finite; a program needn't handle non-finite values.
Results may differ from a plain program's by a relative error of at most 0.006.
Values may be sent and summed in bfloat16 or wider, within the bound.
A program may use at most 64 MiB of HBM per device.

v0:
```python
import functools
import math

import jax
import jax.numpy as jnp
from jax import lax
from jax.experimental import pallas as pl
from jax.experimental.pallas import tpu as pltpu
from jax.sharding import PartitionSpec as P

BLK = 128
CAP = 2


def partner_2(x, axis, distance):
    return lax.ppermute(x, axis, [(i, i ^ 1 << distance) for i in range(lax.axis_size(axis))])


def parity_table(count):
    index = jnp.arange(count, dtype=jnp.int32)
    total = jnp.zeros((count, count), jnp.int32)
    for level in range(count.bit_length() - 1):
        total = total + (
            jnp.right_shift(index[:, None], level) & jnp.right_shift(index[None, :], level) & 1
        )
    return (1 - 2 * (total % 2)).astype(jnp.float32)


def route_sampled(mixed, block_ids, me_index, shards, blocks_per, tokens, width):
    groups = block_ids.shape[1] // CAP
    sources = block_ids[:, ::CAP] // blocks_per
    local_ids = (block_ids % blocks_per).reshape(shards, groups, CAP)
    matched = sources == me_index
    chosen = jnp.sum(jnp.where(matched[:, :, None], local_ids, 0), axis=1)
    live_rows = jnp.any(matched, axis=1).astype(jnp.bfloat16)
    outgoing = jnp.take(mixed, chosen.reshape(-1), axis=0).reshape(shards, CAP, tokens, width)
    return (outgoing * live_rows[:, None, None, None], jnp.take(sources, me_index, axis=0))


def body(activations, out_grads, sign_bits, block_ids):
    shards = lax.axis_size("shard")
    me_index = lax.axis_index("shard")
    tokens = out_grads.shape[0]
    width = BLK
    own_blocks = block_ids.shape[1]
    blocks_per = out_grads.shape[1] // width
    model_width = activations.shape[1] * shards
    inv_block = 1.0 / math.sqrt(width)
    inv_shard = 1.0 / math.sqrt(shards)
    partial_gram = jnp.dot(activations, activations.T, preferred_element_type=jnp.float32)
    token_gram = lax.psum(partial_gram, "shard").astype(jnp.bfloat16)
    sign_values = (1 - 2 * sign_bits).astype(jnp.bfloat16)
    flipped = (out_grads * sign_values[None, :]).reshape(tokens, blocks_per, width)
    block_table = parity_table(width).astype(jnp.bfloat16)
    local_mix = jnp.einsum("tbj,jk->btk", flipped, block_table, preferred_element_type=jnp.float32)
    local_mix = (local_mix * inv_block).astype(jnp.bfloat16)
    running = local_mix.astype(jnp.float32)
    for level in range(shards.bit_length() - 1):
        partner = partner_2(running, "shard", level)
        upper = jnp.right_shift(me_index, level) & 1 == 1
        running = jnp.where(upper, partner - running, running + partner)
    mixed = (running * inv_shard).astype(jnp.bfloat16)
    outgoing, own_sources = route_sampled(
        mixed, block_ids, me_index, shards, blocks_per, tokens, width
    )
    incoming = lax.all_to_all(outgoing, "shard", split_axis=0, concat_axis=0, tiled=True)
    sketched = jnp.take(incoming, own_sources, axis=0).reshape(own_blocks, tokens, width)
    weighted = jnp.einsum(
        "tu,jub->jtb", token_gram, sketched, preferred_element_type=jnp.float32
    ).astype(jnp.bfloat16)
    block_gram = jnp.einsum("jtb,ktc->jbkc", sketched, weighted, preferred_element_type=jnp.float32)
    own_cols = own_blocks * width
    block_gram = block_gram.reshape(own_cols, own_cols)
    summed = lax.psum(block_gram, "dp")
    return summed / (lax.axis_size("dp") * tokens * model_width)


ALONG = pl.DeviceIdType.MESH
SPANS = ((0, 2), (2, 4), (4, 6), (6, 7), (7, 8))
CHUNKS = len(SPANS)
FIRST = tuple(sum((hi - lo) * hi for lo, hi in SPANS[:c]) for c in range(CHUNKS + 1))
UNITS = FIRST[CHUNKS]
TRIANGLE = tuple((i, j) for i in range(4) for j in range(i + 1))
GSPANS = ((0, 2), (2, 4), (4, 6), (6, 8), (8, 10))
GS = len(GSPANS)
CUTS = 4


def pick_kernel(shards, own, per, ids, bits, grads, out):
    z = lax.axis_index("shard")
    width = BLK
    number = shards * own

    def start_of(p):
        block = ids[p // own, lax.rem(p, own)]
        r = block // per
        return r, pl.multiple_of((block - r * per) * width, width)

    def take(p, carry):
        r, start = start_of(p)
        common = r & z
        odd = common & 1
        for level in range(1, shards.bit_length() - 1):
            odd = odd + ((common >> level) & 1)
        sign = 1 - 2 * (odd & 1)
        signs = ((1 - 2 * bits[pl.ds(start, width)].reshape(1, width)) * sign).astype(jnp.float32).astype(jnp.bfloat16)
        out[p] = grads[:, pl.ds(start, width)] * signs
        return carry

    lax.fori_loop(0, number, take, 0, unroll=4)


def mix_kernel(
    shards, parts, own, act, picked, out,
    rx, tx, grx, gtx, part, full, sketch, halves, prx, rtx, rrx, gathered,
    z_send, z_recv, p_send, p_recv, r_send, r_recv, f_send, f_recv, a_send, a_recv, w_send, w_recv,
):
    z = lax.axis_index("shard")
    d = lax.axis_index("dp")
    core = lax.rem(d, 2)
    chip = d // 2
    last = shards - 1
    edge = (z == 0) | (z == last)
    middle = jnp.logical_not(edge)
    tokens = act.shape[0]
    width = BLK
    inv_block = 1.0 / math.sqrt(width)
    inv_shard = 1.0 / math.sqrt(shards)
    pieces = 2 * own

    barrier = pltpu.get_barrier_semaphore()

    def peer(m):
        flipped = 1 - lax.rem(chip, 2) if m & 1 else lax.rem(chip, 2)
        high = 1 - chip // 2 if m & 2 else chip // 2
        return (high * 2 + flipped) * 2 + core

    partner = chip * 2 + 1 - core
    for m in (1, 2, 3):
        pl.semaphore_signal(barrier, inc=1, device_id={"dp": peer(m)}, device_id_type=ALONG)
    pl.semaphore_signal(barrier, inc=1, device_id={"dp": partner}, device_id_type=ALONG)

    @pl.when(z > 0)
    def _():
        pl.semaphore_signal(barrier, inc=1, device_id={"shard": z - 1}, device_id_type=ALONG)

    @pl.when(z < last)
    def _():
        pl.semaphore_signal(barrier, inc=1, device_id={"shard": z + 1}, device_id_type=ALONG)

    row = lax.broadcasted_iota(jnp.int32, (width, width), 0)
    col = lax.broadcasted_iota(jnp.int32, (width, width), 1)
    both = row & col
    count = both & 1
    for level in range(1, width.bit_length() - 1):
        count = count + ((both >> level) & 1)
    table = (1 - 2 * (count & 1)).astype(jnp.float32).astype(jnp.bfloat16)

    def contribution(owner, j):
        lm = jnp.dot(picked[owner * own + j], table, preferred_element_type=jnp.float32)
        return (lm * inv_block).astype(jnp.bfloat16).astype(jnp.float32) * inv_shard

    def owner_of(way, t):
        return jnp.where(way == 0, 1 - t, 2 + t)

    def target(way):
        return jnp.where(way == 0, z - 1, z + 1)

    half = tokens // CUTS

    def s_move(way, k, h, who):
        rows = pl.ds(half * h, half)
        return pltpu.make_async_remote_copy(
            tx.at[way, k, rows], rx.at[way, k, rows], z_send.at[way, GS + CUTS * k + h], z_recv.at[way, GS + CUTS * k + h],
            device_id={"shard": who}, device_id_type=ALONG)

    def s_copy(way, k, h):
        return s_move(way, k, h, target(way))

    def g_copy(way, i):
        lo, hi = GSPANS[i]
        return pltpu.make_async_remote_copy(
            gtx.at[way, lo:hi], grx.at[way, lo:hi], z_send.at[way, i], z_recv.at[way, i],
            device_id={"shard": target(way)}, device_id_type=ALONG)

    def gpart(n):
        i, j = TRIANGLE[n]
        return part[128 * i : 128 * (i + 1), 128 * j : 128 * (j + 1)]

    def units(c):
        return pl.ds(FIRST[c], FIRST[c + 1] - FIRST[c])

    def a_copy(c, slot, who):
        return pltpu.make_async_remote_copy(
            gathered.at[d, units(c)], gathered.at[d, units(c)], a_send.at[c, slot], a_recv.at[c, slot],
            device_id={"dp": who}, device_id_type=ALONG)

    def a_recv_from(c, slot, who):
        return pltpu.make_async_remote_copy(
            gathered.at[who, units(c)], gathered.at[who, units(c)], a_send.at[c, slot], a_recv.at[c, slot],
            device_id={"dp": who}, device_id_type=ALONG)

    def w_copy(c, m):
        return pltpu.make_async_remote_copy(
            gathered.at[peer(m), units(c)], gathered.at[peer(m), units(c)],
            w_send.at[c, m - 1], w_recv.at[c, m - 1],
            device_id={"dp": partner}, device_id_type=ALONG)

    def w_recv_from(c, m):
        other = peer(m) + 1 - 2 * core
        return pltpu.make_async_remote_copy(
            gathered.at[other, units(c)], gathered.at[other, units(c)],
            w_send.at[c, m - 1], w_recv.at[c, m - 1],
            device_id={"dp": partner}, device_id_type=ALONG)

    def spread(c):
        for m in (1, 2, 3):
            a_copy(c, m - 1, peer(m)).start()
        a_copy(c, 3, partner).start()

    def relay(c):
        for m in (1, 2, 3):
            a_recv_from(c, m - 1, peer(m)).wait_recv()
            w_copy(c, m).start()

    def settle(c):
        a_recv_from(c, 3, partner).wait_recv()
        for m in (1, 2, 3):
            w_recv_from(c, m).wait_recv()
        for m in (1, 2, 3):
            a_copy(c, m - 1, peer(m)).wait_send()
            w_copy(c, m).wait_send()
        a_copy(c, 3, partner).wait_send()

    def f_copy(c):
        inward = jnp.where(z == 0, 1, last - 1)
        return pltpu.make_async_remote_copy(
            rrx.at[3, units(c)], gathered.at[d, units(c)], f_send.at[c], f_recv.at[c],
            device_id={"shard": inward}, device_id_type=ALONG)

    def f_recv_at():
        def make(c):
            outward = jnp.where(z == 1, 0, last)
            return pltpu.make_async_remote_copy(
                rrx.at[3, units(c)], gathered.at[d, units(c)], f_send.at[c], f_recv.at[c],
                device_id={"shard": outward}, device_id_type=ALONG)
        return make

    part[...] = lax.dot_general(act[...], act[...], (((1,), (1,)), ((), ())), preferred_element_type=jnp.float32)

    @pl.when(edge)
    def _():
        pl.semaphore_wait(barrier, 5)

    @pl.when(middle)
    def _():
        pl.semaphore_wait(barrier, 6)

    @pl.when(edge)
    def _():
        out_way = jnp.where(z == 0, 1, 0)
        in_way = 1 - out_way
        for i in range(GS):
            for n in range(*GSPANS[i]):
                gtx[out_way, n] = gpart(n).astype(jnp.bfloat16)
            g_copy(out_way, i).start()

        def push(k, carry):
            t, j = k // own, lax.rem(k, own)
            tx[out_way, k] = contribution(owner_of(out_way, t), j).astype(jnp.bfloat16)
            for h in range(CUTS):
                s_copy(out_way, k, h).start()
            return carry

        lax.fori_loop(0, pieces, push, 0)

        for i in range(GS):
            lo, hi = GSPANS[i]
            pltpu.make_async_remote_copy(
                gtx.at[in_way, lo:hi], grx.at[in_way, lo:hi], z_send.at[in_way, i], z_recv.at[in_way, i],
                device_id={"shard": target(out_way)}, device_id_type=ALONG).wait_recv()
            for n in range(lo, hi):
                r, c = TRIANGLE[n]
                block = (grx[in_way, n].astype(jnp.float32) + gpart(n)).astype(jnp.bfloat16)
                full[128 * r : 128 * (r + 1), 128 * c : 128 * (c + 1)] = block
                if r != c:
                    full[128 * c : 128 * (c + 1), 128 * r : 128 * (r + 1)] = block.T

        def where(q):
            t, c = q // CHUNKS, q % CHUNKS
            return t, c, pl.ds(UNITS * t + FIRST[c], FIRST[c + 1] - FIRST[c])

        def p_copy(q):
            t, c, us = where(q)
            return pltpu.make_async_remote_copy(
                halves.at[1 - core, us], prx.at[us], p_send.at[q], p_recv.at[q],
                device_id={"dp": partner}, device_id_type=ALONG)

        def r_copy(q, m):
            t, c, us = where(q)
            return pltpu.make_async_remote_copy(
                rtx.at[peer(m) // 2, us], rrx.at[m - 1, us], r_send.at[q, m - 1], r_recv.at[q, m - 1],
                device_id={"dp": peer(m)}, device_id_type=ALONG)

        def step_a(q):
            t, c, us = where(q)
            lo, hi = SPANS[c]
            for j in range(lo, hi):
                k = own * t + j
                mine = contribution(owner_of(in_way, t), j)
                for h in range(CUTS):
                    s_move(in_way, k, h, target(out_way)).wait_recv()
                done = (rx[in_way, k].astype(jnp.float32) + mine).astype(jnp.bfloat16)
                sketch[t, :, width * j : width * (j + 1)] = done
            cols = sketch[t, :, width * lo : width * hi]
            weighted = jnp.dot(full[...], cols, preferred_element_type=jnp.float32).astype(jnp.bfloat16)
            for top in range(0, hi, 2):
                end = min(top + 2, hi)
                unit = lax.dot_general(
                    sketch[t, :, width * top : width * end], weighted, (((0,), (0,)), ((), ())),
                    preferred_element_type=jnp.float32)
                for i in range(top, end):
                    for j in range(lo, hi):
                        u = UNITS * t + FIRST[c] + (j - lo) * hi + i
                        block = unit[128 * (i - top) : 128 * (i - top + 1), width * (j - lo) : width * (j - lo + 1)]
                        halves[0, u] = block[:64]
                        halves[1, u] = block[64:]
            p_copy(q).start()

        def step_b(q):
            t, c, us = where(q)
            p_copy(q).wait_recv()
            total = (halves[core, us] + prx[us]).astype(jnp.bfloat16)
            for n in range(4):
                rtx[n, us] = total[:, 16 * n : 16 * (n + 1)]
            for m in (1, 2, 3):
                r_copy(q, m).start()

        def step_c(q):
            t, c, us = where(q)
            for m in (1, 2, 3):
                r_copy(q, m).wait_recv()
            total = rtx[chip, us].astype(jnp.float32)
            for m in range(3):
                total = total + rrx[m, us].astype(jnp.float32)
            total = (total * (1.0 / (parts * tokens * act.shape[1] * shards))).astype(jnp.bfloat16)
            if t == 0:
                rrx[3, units(c)] = total
            else:
                gathered[d, units(c)] = total
            if t == 0:
                f_copy(c).start()
            else:
                spread(c)

        def step_d(q):
            if q >= CHUNKS:
                relay(q - CHUNKS)

        steps = 2 * CHUNKS
        for q in range(steps + 3):
            if 0 <= q - 1 < steps:
                step_b(q - 1)
            if 0 <= q - 2 < steps:
                step_c(q - 2)
            if 0 <= q - 3 < steps:
                step_d(q - 3)
            if q < steps:
                step_a(q)
        for c in range(CHUNKS):
            settle(c)
            f_copy(c).wait_send()
        for q in range(steps):
            p_copy(q).wait_send()
            for m in (1, 2, 3):
                r_copy(q, m).wait_send()
        for i in range(GS):
            g_copy(out_way, i).wait_send()

        def drain(k, carry):
            for h in range(CUTS):
                s_copy(out_way, k, h).wait_send()
            return carry

        lax.fori_loop(0, pieces, drain, 0)

    @pl.when(middle)
    def _():
        near = jnp.where(z == 1, 1, 0)
        far = 1 - near

        def pass_g(way, i):
            g_copy(way, i).wait_recv()
            for n in range(*GSPANS[i]):
                gtx[way, n] = (grx[way, n].astype(jnp.float32) + gpart(n)).astype(jnp.bfloat16)
            g_copy(way, i).start()

        def pass_s(way, k):
            t, j = k // own, lax.rem(k, own)
            mine = contribution(owner_of(way, t), j)
            for h in range(CUTS):
                s_copy(way, k, h).wait_recv()
                rows = slice(half * h, half * (h + 1))
                tx[way, k, rows] = (rx[way, k, rows].astype(jnp.float32) + mine[rows]).astype(jnp.bfloat16)
                s_copy(way, k, h).start()

        for i in range(GS):
            pass_g(near, i)
            if i >= 2:
                pass_g(far, i - 2)
        pass_s(near, 0)
        pass_g(far, GS - 2)
        pass_g(far, GS - 1)

        def both_ways(k, carry):
            pass_s(near, k)
            pass_s(far, k - 1)
            return carry

        lax.fori_loop(1, pieces, both_ways, 0)
        pass_s(far, pieces - 1)
        arrival = f_recv_at()
        for c in range(CHUNKS):
            arrival(c).wait_recv()
            spread(c)
        for c in range(CHUNKS):
            relay(c)
        for c in range(CHUNKS):
            settle(c)
        for way in range(2):
            for i in range(GS):
                g_copy(way, i).wait_send()

        def drain(k, carry):
            for way in range(2):
                for h in range(CUTS):
                    s_copy(way, k, h).wait_send()
            return carry

        lax.fori_loop(0, pieces, drain, 0)

    out[...] = gathered[...]


def assemble_kernel(got, out, held, sems):
    chunk_of = [c for c, (lo, hi) in enumerate(SPANS) for _ in range(lo, hi)]

    def unit(i, j):
        c = chunk_of[j]
        lo, hi = SPANS[c]
        u = FIRST[c] + (j - lo) * hi + i
        rows = [got[2 * n + h, u] for h in range(2) for n in range(4)]
        return jnp.concatenate(rows, axis=0).astype(jnp.float32)

    count = len(chunk_of)

    def put(i):
        rows = pl.ds(BLK * i, BLK)
        return pltpu.make_async_copy(held.at[rows], out.at[rows], sems.at[i])

    for i in range(count):
        for j in range(count):
            block = unit(i, j) if i < SPANS[chunk_of[j]][1] else unit(j, i).T
            held[BLK * i : BLK * (i + 1), BLK * j : BLK * (j + 1)] = block
        put(i).start()
    for i in range(count):
        put(i).wait()


def fast_body(shards, parts, activations, out_grads, sign_bits, block_ids):
    tokens, columns = out_grads.shape
    per = columns // BLK
    own = block_ids.shape[1]
    vmem = pl.BlockSpec(memory_space=pltpu.VMEM)
    bf, f32 = jnp.bfloat16, jnp.float32
    dma = pltpu.SemaphoreType.DMA
    number = shards * own
    hbm = pl.BlockSpec(memory_space=pltpu.HBM)
    picked = pl.pallas_call(
        functools.partial(pick_kernel, shards, own, per),
        out_shape=jax.ShapeDtypeStruct((number, tokens, BLK), bf),
        in_specs=[pl.BlockSpec(memory_space=pltpu.SMEM), vmem, vmem],
        out_specs=vmem,
        compiler_params=pltpu.CompilerParams(vmem_limit_bytes=12 * 2**20),
        name="pick",
    )(block_ids, sign_bits, out_grads)
    got = pl.pallas_call(
        functools.partial(mix_kernel, shards, parts, own),
        out_shape=jax.ShapeDtypeStruct((parts, UNITS, 16, BLK), bf),
        in_specs=[vmem, vmem],
        out_specs=vmem,
        scratch_shapes=[
            pltpu.VMEM((2, 2 * own, tokens, BLK), bf),
            pltpu.VMEM((2, 2 * own, tokens, BLK), bf),
            pltpu.VMEM((2, 10, 128, 128), bf),
            pltpu.VMEM((2, 10, 128, 128), bf),
            pltpu.VMEM((tokens, tokens), f32),
            pltpu.VMEM((tokens, tokens), bf),
            pltpu.VMEM((2, tokens, own * BLK), bf),
            pltpu.VMEM((2, 2 * UNITS, 64, BLK), f32),
            pltpu.VMEM((2 * UNITS, 64, BLK), f32),
            pltpu.VMEM((4, 2 * UNITS, 16, BLK), bf),
            pltpu.VMEM((4, 2 * UNITS, 16, BLK), bf),
            pltpu.VMEM((parts, UNITS, 16, BLK), bf),
            dma((2, GS + 2 * CUTS * own)), dma((2, GS + 2 * CUTS * own)),
            dma((2 * CHUNKS,)), dma((2 * CHUNKS,)),
            dma((2 * CHUNKS, 3)), dma((2 * CHUNKS, 3)),
            dma((CHUNKS,)), dma((CHUNKS,)),
            dma((CHUNKS, 4)), dma((CHUNKS, 4)),
            dma((CHUNKS, 3)), dma((CHUNKS, 3)),
        ],
        compiler_params=pltpu.CompilerParams(collective_id=0, has_side_effects=True, vmem_limit_bytes=40 * 2**20),
        name="mix",
    )(activations, picked)
    return pl.pallas_call(
        assemble_kernel,
        out_shape=jax.ShapeDtypeStruct((own * BLK, own * BLK), f32),
        in_specs=[vmem],
        out_specs=hbm,
        scratch_shapes=[pltpu.VMEM((own * BLK, own * BLK), f32), dma((own,))],
        compiler_params=pltpu.CompilerParams(vmem_limit_bytes=16 * 2**20),
        name="assemble",
    )(got)


def solution(mesh):
    in_specs = (P("dp", "shard"), P("dp", "shard"), P("shard"), P())
    out_specs = P("shard", None)
    shards, parts = mesh.shape["shard"], mesh.shape["dp"]
    chosen = functools.partial(fast_body, shards, parts) if (shards, parts) == (4, 8) else body
    return jax.shard_map(chosen, mesh=mesh, in_specs=in_specs, out_specs=out_specs, check_vma=False)
```

profile of v0, /device:TPU:0, one launch (start us, length us, event | category | flops | bytes accessed | tf_op | source)
XLA Modules:
  0.0 91.2 jit_solution(303508766631036425)
XLA Ops:
  0.0 0.0 copy-start
  0.0 2.0 %copy-done = bf16[512,3584]{1,0:T(8,128)(2,1)S(1)} copy-done((bf16[512,3584]{1,0:T(8,128)(2,1)S(1)}, bf16[512,3584]{1,0:T(8,128)(2,1)}, u32[]{:S(2)}) %copy-start) | copy-done | bytes 3670040
  2.0 0.0 copy-start.2
  2.0 0.7 copy-done.2
  2.8 0.0 copy-start.3
  2.8 0.7 copy-done.3
  3.4 0.0 copy-start.1
  3.4 1.5 %pick.1.picked = bf16[32,512,128]{2,1,0:T(8,128)(2,1)S(1)} custom-call(s32[4,8]{1,0:T(4,128)S(1)} %copy-done.3, s32[3584]{0:T(1024)S(1)} %copy-done.2, bf16[512,3584]{1,0:T(8,128)(2,1)S(1)} %copy-done), custom_call_target="tpu_custom_call" | custom-call | tf_op jit(solution)/shard_map/pick/pallas_call | solution.py:479
  4.9 0.0 copy-done.1
  4.9 84.2 %mix.1.got = bf16[8,39,16,128]{3,2,1,0:T(8,128)(2,1)S(1)} custom-call(bf16[512,1024]{1,0:T(8,128)(2,1)S(1)} %copy-done.1, bf16[32,512,128]{2,1,0:T(8,128)(2,1)S(1)} %pick.1.picked), custom_call_target="tpu_custom_call" | custom-call | tf_op jit(solution)/shard_map/mix/pallas_call | solution.py:487
  89.1 2.1 %assemble.1 = f32[1024,1024]{1,0:T(8,128)} custom-call(bf16[8,39,16,128]{3,2,1,0:T(8,128)(2,1)S(1)} %mix.1.got), custom_call_target="tpu_custom_call" | custom-call | tf_op jit(solution)/shard_map/assemble/pallas_call | solution.py:515
Async XLA Ops:
  0.0 2.0 %copy-start = (bf16[512,3584]{1,0:T(8,128)(2,1)S(1)}, bf16[512,3584]{1,0:T(8,128)(2,1)}, u32[]{:S(2)}) copy-start(bf16[512,3584]{1,0:T(8,128)(2,1)} %grads.1) | copy-start | bytes 11010052
  2.0 0.7 copy-start.2
  2.8 0.7 copy-start.3
  3.4 1.5 %copy-start.1 = (bf16[512,1024]{1,0:T(8,128)(2,1)S(1)}, bf16[512,1024]{1,0:T(8,128)(2,1)}, u32[]{:S(2)}) copy-start(bf16[512,1024]{1,0:T(8,128)(2,1)} %act.1) | copy-start | bytes 3145732
where the time goes:
time: 91.5 us; the launch traced here: 91.2 us
  Pallas kernels  87.8 us (96%)
  local copies, waits for them, and re-layouts  3.44 us (4%)
    pallas_call x1, Pallas kernels, fast_body(): pl.pallas_call(functools.partial(mix_kernel, shards, parts, own), out_sha...  84.2 us
    unnamed x8, local copies, waits for them, and re-layouts  3.44 us
    pallas_call x1, Pallas kernels, fast_body(): pl.pallas_call(assemble_kernel, out_shape=jax.ShapeDtypeStruct((own * BLK...  2.13 us

commit v1 on v0

v1 whole, which is shorter than its diff:
```python
import functools
import math

import jax
import jax.numpy as jnp
from jax import lax
from jax.experimental import pallas as pl
from jax.experimental.pallas import tpu as pltpu
from jax.sharding import PartitionSpec as P

BLK = 128
CAP = 2


def partner_2(x, axis, distance):
    return lax.ppermute(x, axis, [(i, i ^ 1 << distance) for i in range(lax.axis_size(axis))])


def parity_table(count):
    index = jnp.arange(count, dtype=jnp.int32)
    total = jnp.zeros((count, count), jnp.int32)
    for level in range(count.bit_length() - 1):
        total = total + (
            jnp.right_shift(index[:, None], level) & jnp.right_shift(index[None, :], level) & 1
        )
    return (1 - 2 * (total % 2)).astype(jnp.float32)


def route_sampled(mixed, block_ids, me_index, shards, blocks_per, tokens, width):
    groups = block_ids.shape[1] // CAP
    sources = block_ids[:, ::CAP] // blocks_per
    local_ids = (block_ids % blocks_per).reshape(shards, groups, CAP)
    matched = sources == me_index
    chosen = jnp.sum(jnp.where(matched[:, :, None], local_ids, 0), axis=1)
    live_rows = jnp.any(matched, axis=1).astype(jnp.bfloat16)
    outgoing = jnp.take(mixed, chosen.reshape(-1), axis=0).reshape(shards, CAP, tokens, width)
    return (outgoing * live_rows[:, None, None, None], jnp.take(sources, me_index, axis=0))


def body(activations, out_grads, sign_bits, block_ids):
    shards = lax.axis_size("shard")
    me_index = lax.axis_index("shard")
    tokens = out_grads.shape[0]
    width = BLK
    own_blocks = block_ids.shape[1]
    blocks_per = out_grads.shape[1] // width
    model_width = activations.shape[1] * shards
    inv_block = 1.0 / math.sqrt(width)
    inv_shard = 1.0 / math.sqrt(shards)
    partial_gram = jnp.dot(activations, activations.T, preferred_element_type=jnp.float32)
    token_gram = lax.psum(partial_gram, "shard").astype(jnp.bfloat16)
    sign_values = (1 - 2 * sign_bits).astype(jnp.bfloat16)
    flipped = (out_grads * sign_values[None, :]).reshape(tokens, blocks_per, width)
    block_table = parity_table(width).astype(jnp.bfloat16)
    local_mix = jnp.einsum("tbj,jk->btk", flipped, block_table, preferred_element_type=jnp.float32)
    local_mix = (local_mix * inv_block).astype(jnp.bfloat16)
    running = local_mix.astype(jnp.float32)
    for level in range(shards.bit_length() - 1):
        partner = partner_2(running, "shard", level)
        upper = jnp.right_shift(me_index, level) & 1 == 1
        running = jnp.where(upper, partner - running, running + partner)
    mixed = (running * inv_shard).astype(jnp.bfloat16)
    outgoing, own_sources = route_sampled(
        mixed, block_ids, me_index, shards, blocks_per, tokens, width
    )
    incoming = lax.all_to_all(outgoing, "shard", split_axis=0, concat_axis=0, tiled=True)
    sketched = jnp.take(incoming, own_sources, axis=0).reshape(own_blocks, tokens, width)
    weighted = jnp.einsum(
        "tu,jub->jtb", token_gram, sketched, preferred_element_type=jnp.float32
    ).astype(jnp.bfloat16)
    block_gram = jnp.einsum("jtb,ktc->jbkc", sketched, weighted, preferred_element_type=jnp.float32)
    own_cols = own_blocks * width
    block_gram = block_gram.reshape(own_cols, own_cols)
    summed = lax.psum(block_gram, "dp")
    return summed / (lax.axis_size("dp") * tokens * model_width)


ALONG = pl.DeviceIdType.MESH
COUNT = 8
PIECES = 2 * COUNT
CUTS = 4
GB = 10
TRIANGLE = tuple((i, j) for i in range(4) for j in range(i + 1))
UNITS = COUNT * (COUNT + 1) // 2
ORDER = tuple((1, COUNT - 1) if k == PIECES - 1 else (0, (k + 1) // 2) if k % 2 or k == 0 else (1, k // 2 - 1) for k in range(PIECES))
WHOLE = tuple((j, 0, BLK) for j in range(COUNT))
SPLIT = WHOLE[:-1] + ((COUNT - 1, 0, BLK // 2), (COUNT - 1, BLK // 2, BLK))
CHUNKS = (WHOLE, SPLIT)
STEPS = tuple((t, c, k) for k, (t, j) in enumerate(ORDER) for c, chunk in enumerate(CHUNKS[t]) if chunk[0] == j)


def units_of(chunk):
    j, lo, hi = chunk
    first = j * (j + 1) // 2
    if j < COUNT - 1:
        return first, j + 1
    half = COUNT // 2
    return first + half * (lo // (BLK // 2)), half * ((hi - lo) // (BLK // 2))


def mix_kernel(
    shards, parts, own, per, act_hbm, grads_hbm, bits_hbm, ids_hbm, gathered,
    act, grads, bits, flips, ids, rx, tx, grx, gtx, part, full, sketch, keep, give, prx, rtx, rrx,
    l_sem, z_send, z_recv, p_send, p_recv, r_send, r_recv, f_send, f_recv, a_send, a_recv, w_send, w_recv,
):
    z = lax.axis_index("shard")
    d = lax.axis_index("dp")
    core = lax.rem(d, 2)
    chip = d // 2
    last = shards - 1
    edge = (z == 0) | (z == last)
    middle = jnp.logical_not(edge)
    tokens = act.shape[0]
    width = BLK
    inv_block = 1.0 / math.sqrt(width)
    inv_shard = 1.0 / math.sqrt(shards)
    quarter = width // CUTS

    barrier = pltpu.get_barrier_semaphore()

    def peer(m):
        flipped = 1 - lax.rem(chip, 2) if m & 1 else lax.rem(chip, 2)
        high = 1 - chip // 2 if m & 2 else chip // 2
        return (high * 2 + flipped) * 2 + core

    partner = chip * 2 + 1 - core
    for m in (1, 2, 3):
        pl.semaphore_signal(barrier, inc=1, device_id={"dp": peer(m)}, device_id_type=ALONG)
    pl.semaphore_signal(barrier, inc=1, device_id={"dp": partner}, device_id_type=ALONG)

    @pl.when(z > 0)
    def _():
        pl.semaphore_signal(barrier, inc=1, device_id={"shard": z - 1}, device_id_type=ALONG)

    @pl.when(z < last)
    def _():
        pl.semaphore_signal(barrier, inc=1, device_id={"shard": z + 1}, device_id_type=ALONG)

    loads = (
        pltpu.make_async_copy(act_hbm, act, l_sem.at[0]),
        pltpu.make_async_copy(ids_hbm, ids, l_sem.at[1]),
        pltpu.make_async_copy(bits_hbm, bits, l_sem.at[2]),
    ) + tuple(
        pltpu.make_async_copy(grads_hbm.at[:, pl.ds(width * b, width)], grads.at[b], l_sem.at[3 + b]) for b in range(per)
    )
    for load in loads:
        load.start()

    row = lax.broadcasted_iota(jnp.int32, (width, width), 0)
    col = lax.broadcasted_iota(jnp.int32, (width, width), 1)
    both = row & col
    count = both & 1
    for level in range(1, width.bit_length() - 1):
        count = count + ((both >> level) & 1)
    table = (1 - 2 * (count & 1)).astype(jnp.float32)

    def contribution(owner, j):
        block = ids[owner, j]
        r = lax.div(block, per)
        local = block - r * per
        common = r & z
        odd = common & 1
        for level in range(1, shards.bit_length() - 1):
            odd = odd + ((common >> level) & 1)
        sign = 1 - 2 * (odd & 1)
        signs = flips[local] * sign.astype(jnp.float32)
        lm = lax.dot_general(
            (table * signs).astype(jnp.bfloat16), grads[local], (((1,), (1,)), ((), ())),
            preferred_element_type=jnp.float32)
        return ((lm * inv_block).astype(jnp.bfloat16).astype(jnp.float32) * inv_shard).astype(jnp.bfloat16)

    def owner_of(way, t):
        return jnp.where(way == 0, 1 - t, 2 + t)

    def piece(k):
        if isinstance(k, int):
            return ORDER[k]
        odd = lax.rem(k, 2) == 1
        final = k == PIECES - 1
        t = jnp.where(final | jnp.logical_not(odd | (k == 0)), 1, 0)
        j = jnp.where(final, COUNT - 1, jnp.where(t == 1, k // 2 - 1, (k + 1) // 2))
        return t, j

    def target(way):
        return jnp.where(way == 0, z - 1, z + 1)

    def s_move(way, k, h, who):
        rows = pl.ds(quarter * h, quarter)
        n = GB + CUTS * k + h
        return pltpu.make_async_remote_copy(
            tx.at[way, k, rows], rx.at[way, k, rows], z_send.at[way, n], z_recv.at[way, n],
            device_id={"shard": who}, device_id_type=ALONG)

    def s_copy(way, k, h):
        return s_move(way, k, h, target(way))

    def g_move(way, n, who):
        return pltpu.make_async_remote_copy(
            gtx.at[way, n], grx.at[way, n], z_send.at[way, n], z_recv.at[way, n],
            device_id={"shard": who}, device_id_type=ALONG)

    def g_copy(way, n):
        return g_move(way, n, target(way))

    def gpart(n):
        i, j = TRIANGLE[n]
        return part[128 * i : 128 * (i + 1), 128 * j : 128 * (j + 1)]

    def fill(way, k):
        t, j = piece(k)
        tx[way, k] = contribution(owner_of(way, t), j)

    def units(t, c):
        return pl.ds(*units_of(CHUNKS[t][c]))

    def a_move(t, c, slot, who, holder):
        return pltpu.make_async_remote_copy(
            gathered.at[holder, units(t, c)], gathered.at[holder, units(t, c)], a_send.at[c, slot], a_recv.at[c, slot],
            device_id={"dp": who}, device_id_type=ALONG)

    def w_move(t, c, m, holder):
        return pltpu.make_async_remote_copy(
            gathered.at[holder, units(t, c)], gathered.at[holder, units(t, c)],
            w_send.at[c, m - 1], w_recv.at[c, m - 1],
            device_id={"dp": partner}, device_id_type=ALONG)

    def spread(t, c):
        for m in (1, 2, 3):
            a_move(t, c, m - 1, peer(m), d).start()
        a_move(t, c, 3, partner, d).start()

    def relay(t, c):
        for m in (1, 2, 3):
            a_move(t, c, m - 1, peer(m), peer(m)).wait_recv()
            w_move(t, c, m, peer(m)).start()

    def settle(t, c):
        a_move(t, c, 3, partner, partner).wait_recv()
        for m in (1, 2, 3):
            w_move(t, c, m, peer(m) + 1 - 2 * core).wait_recv()
        for m in (1, 2, 3):
            a_move(t, c, m - 1, peer(m), d).wait_send()
            w_move(t, c, m, peer(m)).wait_send()
        a_move(t, c, 3, partner, d).wait_send()

    def f_copy(c, who):
        us = units(0, c)
        return pltpu.make_async_remote_copy(
            rrx.at[3, us], gathered.at[d, us], f_send.at[c], f_recv.at[c],
            device_id={"shard": who}, device_id_type=ALONG)

    loads[0].wait()
    part[...] = lax.dot_general(act[...], act[...], (((1,), (1,)), ((), ())), preferred_element_type=jnp.float32)
    for load in loads[1:]:
        load.wait()
    for b in range(per):
        flips[b] = (1 - 2 * bits[width * b : width * (b + 1)].reshape(1, width)).astype(jnp.float32)

    @pl.when(edge)
    def _():
        pl.semaphore_wait(barrier, 5)

    @pl.when(middle)
    def _():
        pl.semaphore_wait(barrier, 6)

    @pl.when(edge)
    def _():
        out_way = jnp.where(z == 0, 1, 0)
        in_way = 1 - out_way
        side = target(out_way)
        for n in range(GB):
            gtx[out_way, n] = gpart(n).astype(jnp.bfloat16)
            g_copy(out_way, n).start()

        def push(k, carry):
            fill(out_way, k)
            for h in range(CUTS):
                s_copy(out_way, k, h).start()
            return carry

        lax.fori_loop(0, PIECES, push, 0)

        def ready(p, carry):
            t, j = p // COUNT, lax.rem(p, COUNT)
            sketch[t, pl.ds(pl.multiple_of(width * j, width), width)] = contribution(owner_of(in_way, t), j)
            return carry

        lax.fori_loop(0, PIECES, ready, 0)

        for n in range(GB):
            g_move(in_way, n, side).wait_recv()
            r, c = TRIANGLE[n]
            block = (grx[in_way, n].astype(jnp.float32) + gpart(n)).astype(jnp.bfloat16)
            full[128 * r : 128 * (r + 1), 128 * c : 128 * (c + 1)] = block
            if r != c:
                full[128 * c : 128 * (c + 1), 128 * r : 128 * (r + 1)] = block.T

        def where(q):
            t, c, k = STEPS[q]
            first, number = units_of(CHUNKS[t][c])
            return t, c, k, pl.ds(UNITS * t + first, number)

        def p_copy(q):
            t, c, k, us = where(q)
            return pltpu.make_async_remote_copy(
                give.at[us], prx.at[us], p_send.at[q], p_recv.at[q],
                device_id={"dp": partner}, device_id_type=ALONG)

        def r_copy(q, m):
            t, c, k, us = where(q)
            return pltpu.make_async_remote_copy(
                rtx.at[peer(m) // 2, us], rrx.at[m - 1, us], r_send.at[q, m - 1], r_recv.at[q, m - 1],
                device_id={"dp": peer(m)}, device_id_type=ALONG)

        def step_a(q):
            t, c, k, us = where(q)
            j, lo, hi = CHUNKS[t][c]
            for h in range(lo // quarter, hi // quarter):
                s_move(in_way, k, h, side).wait_recv()
                rows = slice(width * j + quarter * h, width * j + quarter * (h + 1))
                arrived = rx[in_way, k, quarter * h : quarter * (h + 1)].astype(jnp.float32)
                sketch[t, rows] = (arrived + sketch[t, rows].astype(jnp.float32)).astype(jnp.bfloat16)
            mine = sketch[t, width * j + lo : width * j + hi]
            weighted = jnp.dot(mine, full[...], preferred_element_type=jnp.float32).astype(jnp.bfloat16)
            half = width // 2
            first, number = units_of(CHUNKS[t][c])

            def put(u, top, bottom):
                keep[UNITS * t + u] = jnp.where(core == 0, top, bottom)
                give[UNITS * t + u] = jnp.where(core == 0, bottom, top).astype(jnp.bfloat16)

            for i in range(0, j + 1, 2):
                end = min(i + 2, j + 1)
                block = lax.dot_general(
                    weighted, sketch[t, width * i : width * end], (((1,), (1,)), ((), ())),
                    preferred_element_type=jnp.float32)
                if j < COUNT - 1:
                    for n in range(i, end):
                        cols = slice(width * (n - i), width * (n - i + 1))
                        put(first + n, block[:half, cols], block[half:, cols])
                else:
                    for g in range((hi - lo) // half):
                        rows = slice(half * g, half * (g + 1))
                        put(first + COUNT // 2 * g + i // 2, block[rows, :width], block[rows, width:])
            p_copy(q).start()

        def step_b(q):
            t, c, k, us = where(q)
            p_copy(q).wait_recv()
            total = (keep[us] + prx[us].astype(jnp.float32)).astype(jnp.bfloat16)
            for n in range(4):
                rtx[n, us] = total[:, 16 * n : 16 * (n + 1)]
            for m in (1, 2, 3):
                r_copy(q, m).start()

        def step_c(q):
            t, c, k, us = where(q)
            for m in (1, 2, 3):
                r_copy(q, m).wait_recv()
            total = rtx[chip, us].astype(jnp.float32)
            for m in range(3):
                total = total + rrx[m, us].astype(jnp.float32)
            total = (total * (1.0 / (parts * tokens * act.shape[1] * shards))).astype(jnp.bfloat16)
            if t == 0:
                rrx[3, units(t, c)] = total
                f_copy(c, side).start()
            else:
                gathered[d, units(t, c)] = total
                spread(t, c)

        def step_d(q):
            t, c, k, us = where(q)
            if t == 1:
                relay(t, c)
            p_copy(q).wait_send()
            for m in (1, 2, 3):
                r_copy(q, m).wait_send()

        def drain(k, carry):
            for h in range(CUTS):
                s_copy(out_way, k, h).wait_send()
            return carry

        steps = len(STEPS)
        for q in range(steps - 3):
            step_a(q)
            step_b(q)
            if q >= 2:
                step_c(q - 2)
            if q >= 4:
                step_d(q - 4)
        e = steps - 3
        step_a(e)
        step_c(e - 2)
        step_a(e + 1)
        step_b(e)
        step_a(e + 2)
        step_b(e + 1)
        step_c(e - 1)
        step_b(e + 2)
        step_d(e - 4)
        step_d(e - 3)
        step_d(e - 2)
        step_c(e)
        step_c(e + 1)
        step_c(e + 2)
        for n in range(GB):
            g_copy(out_way, n).wait_send()
        lax.fori_loop(0, PIECES, drain, 0)
        for c in range(len(CHUNKS[1]) - 3):
            settle(1, c)
        step_d(e - 1)
        for c in range(len(CHUNKS[0])):
            f_copy(c, side).wait_send()
        step_d(e)
        step_d(e + 1)
        step_d(e + 2)
        for c in range(len(CHUNKS[1]) - 3, len(CHUNKS[1])):
            settle(1, c)

    @pl.when(middle)
    def _():
        near = jnp.where(z == 1, 1, 0)
        far = 1 - near
        outward = jnp.where(z == 1, 0, last)

        def pass_g(way, n):
            g_copy(way, n).wait_recv()
            gtx[way, n] = (grx[way, n].astype(jnp.float32) + gpart(n)).astype(jnp.bfloat16)
            g_copy(way, n).start()

        def pass_s(way, k, h):
            s_copy(way, k, h).wait_recv()
            rows = slice(quarter * h, quarter * (h + 1))
            tx[way, k, rows] = (rx[way, k, rows].astype(jnp.float32) + tx[way, k, rows].astype(jnp.float32)).astype(jnp.bfloat16)
            s_copy(way, k, h).start()

        lag = CUTS + 1
        for n in range(GB):
            pass_g(near, n)
            if n >= lag:
                pass_g(far, n - lag)
        fill(near, 0)
        for h in range(CUTS):
            pass_s(near, 0, h)
            pass_g(far, GB - lag + h)
        fill(near, 1)
        fill(far, 0)
        pass_s(near, 1, 0)
        pass_g(far, GB - 1)
        for h in range(1, CUTS):
            pass_s(near, 1, h)
            pass_s(far, 0, h - 1)

        def both_ways(k, carry):
            fill(near, k)
            fill(far, k - 1)
            pass_s(near, k, 0)
            pass_s(far, k - 2, CUTS - 1)
            for h in range(1, CUTS):
                pass_s(near, k, h)
                pass_s(far, k - 1, h - 1)
            return carry

        lax.fori_loop(2, PIECES, both_ways, 0)
        fill(far, PIECES - 1)
        pass_s(far, PIECES - 2, CUTS - 1)
        for h in range(CUTS):
            pass_s(far, PIECES - 1, h)

        chunks = len(CHUNKS[0])
        for way in range(2):
            for n in range(GB):
                g_copy(way, n).wait_send()

        def drain(k, carry):
            for h in range(CUTS):
                s_copy(near, k, h).wait_send()
            return carry

        def drain_far(k, carry):
            for h in range(CUTS):
                s_copy(far, k, h).wait_send()
            return carry

        lax.fori_loop(0, PIECES, drain, 0)
        lax.fori_loop(0, PIECES - 2, drain_far, 0)
        for c in range(chunks):
            f_copy(c, outward).wait_recv()
            spread(0, c)
            if c >= 2:
                relay(0, c - 2)
        lax.fori_loop(PIECES - 2, PIECES, drain_far, 0)
        relay(0, chunks - 2)
        for c in range(chunks - 2):
            settle(0, c)
        relay(0, chunks - 1)
        settle(0, chunks - 2)
        settle(0, chunks - 1)


def assemble_kernel(got, out, held, sems):
    half = BLK // 2

    def unit(u):
        rows = [got[2 * n + h, u] for h in range(2) for n in range(4)]
        return jnp.concatenate(rows, axis=0).astype(jnp.float32)

    def put(i):
        rows = pl.ds(BLK * i, BLK)
        return pltpu.make_async_copy(held.at[rows], out.at[rows], sems.at[i])

    final = COUNT - 1
    first = final * COUNT // 2
    lower = {}
    for v in range(COUNT // 2):
        top, bottom = unit(first + v), unit(first + COUNT // 2 + v)
        for g in range(2):
            rows = slice(half * g, half * (g + 1))
            lower[2 * v + g] = jnp.concatenate([top[rows], bottom[rows]], axis=0)
    square = lower[final]
    row = lax.broadcasted_iota(jnp.int32, (BLK, BLK), 0)
    col = lax.broadcasted_iota(jnp.int32, (BLK, BLK), 1)
    lower[final] = jnp.where((row < half) & (col >= half), square.T, square)
    for i in range(COUNT):
        for j in range(COUNT):
            if i == final:
                block = lower[j]
            elif j == final:
                block = lower[i].T
            elif j <= i:
                block = unit(i * (i + 1) // 2 + j)
            else:
                block = unit(j * (j + 1) // 2 + i).T
            held[BLK * i : BLK * (i + 1), BLK * j : BLK * (j + 1)] = block
        put(i).start()
    for i in range(COUNT):
        put(i).wait()


def fast_body(shards, parts, activations, out_grads, sign_bits, block_ids):
    tokens, columns = out_grads.shape
    per = columns // BLK
    own = block_ids.shape[1]
    vmem = pl.BlockSpec(memory_space=pltpu.VMEM)
    hbm = pl.BlockSpec(memory_space=pltpu.HBM)
    bf, f32 = jnp.bfloat16, jnp.float32
    dma = pltpu.SemaphoreType.DMA
    steps, most = len(STEPS), len(CHUNKS[1])
    got = pl.pallas_call(
        functools.partial(mix_kernel, shards, parts, own, per),
        out_shape=jax.ShapeDtypeStruct((parts, UNITS, 16, BLK), bf),
        in_specs=[hbm, hbm, hbm, hbm],
        out_specs=vmem,
        scratch_shapes=[
            pltpu.VMEM(activations.shape, bf),
            pltpu.VMEM((per, tokens, BLK), bf),
            pltpu.VMEM(sign_bits.shape, jnp.int32),
            pltpu.VMEM((per, 1, BLK), f32),
            pltpu.SMEM(block_ids.shape, jnp.int32),
            pltpu.VMEM((2, PIECES, BLK, tokens), bf),
            pltpu.VMEM((2, PIECES, BLK, tokens), bf),
            pltpu.VMEM((2, GB, 128, 128), bf),
            pltpu.VMEM((2, GB, 128, 128), bf),
            pltpu.VMEM((tokens, tokens), f32),
            pltpu.VMEM((tokens, tokens), bf),
            pltpu.VMEM((2, own * BLK, tokens), bf),
            pltpu.VMEM((2 * UNITS, 64, BLK), f32),
            pltpu.VMEM((2 * UNITS, 64, BLK), bf),
            pltpu.VMEM((2 * UNITS, 64, BLK), bf),
            pltpu.VMEM((4, 2 * UNITS, 16, BLK), bf),
            pltpu.VMEM((4, 2 * UNITS, 16, BLK), bf),
            dma((3 + per,)),
            dma((2, GB + CUTS * PIECES)), dma((2, GB + CUTS * PIECES)),
            dma((steps,)), dma((steps,)),
            dma((steps, 3)), dma((steps, 3)),
            dma((COUNT,)), dma((COUNT,)),
            dma((most, 4)), dma((most, 4)),
            dma((most, 3)), dma((most, 3)),
        ],
        compiler_params=pltpu.CompilerParams(collective_id=0, has_side_effects=True, vmem_limit_bytes=40 * 2**20),
        name="mix",
    )(activations, out_grads, sign_bits, block_ids)
    return pl.pallas_call(
        assemble_kernel,
        out_shape=jax.ShapeDtypeStruct((own * BLK, own * BLK), f32),
        in_specs=[vmem],
        out_specs=hbm,
        scratch_shapes=[pltpu.VMEM((own * BLK, own * BLK), f32), dma((own,))],
        compiler_params=pltpu.CompilerParams(vmem_limit_bytes=16 * 2**20),
        name="assemble",
    )(got)


def solution(mesh):
    in_specs = (P("dp", "shard"), P("dp", "shard"), P("shard"), P())
    out_specs = P("shard", None)
    shards, parts = mesh.shape["shard"], mesh.shape["dp"]
    chosen = functools.partial(fast_body, shards, parts) if (shards, parts) == (4, 8) else body
    return jax.shard_map(chosen, mesh=mesh, in_specs=in_specs, out_specs=out_specs, check_vma=False)
```

time: 91.5 us -> 87.3 us (0.954)
  Pallas kernels: 87.8 us -> 82.4 us
  local copies, waits for them, and re-layouts: 3.44 us -> 4.66 us
    pallas_call x2 -> x1, Pallas kernels: 85.6 us -> 80.1 us  [fast_body(): pl.pallas_call(functools.partial(mix_kernel, shards, parts, own, per), ou...]
    unnamed x8, local copies, waits for them, and re-layouts: 3.44 us -> 4.66 us
where the time goes in v1:
time: 87.3 us; the launch traced here: 87.1 us
  Pallas kernels  82.4 us (94%)
  local copies, waits for them, and re-layouts  4.66 us (5%)
    pallas_call x1, Pallas kernels, fast_body(): pl.pallas_call(functools.partial(mix_kernel, shards, parts, own, per), ou...  80.1 us
    unnamed x8, local copies, waits for them, and re-layouts  4.66 us
    pallas_call x1, Pallas kernels, fast_body(): pl.pallas_call(assemble_kernel, out_shape=jax.ShapeDtypeStruct((own * BLK...  2.24 us

profile of v1, /device:TPU:0, one launch (start us, length us, event | category | flops | bytes accessed | tf_op | source)
XLA Modules:
  0.0 87.1 jit_solution(5500603018957981280)
XLA Ops:
  0.0 0.0 copy-start
  0.0 2.0 %copy-done = bf16[512,3584]{1,0:T(8,128)(2,1)S(1)} copy-done((bf16[512,3584]{1,0:T(8,128)(2,1)S(1)}, bf16[512,3584]{1,0:T(8,128)(2,1)}, u32[]{:S(2)}) %copy-start) | copy-done | bytes 3670040
  2.0 0.0 copy-start.1
  2.0 1.2 %copy-done.1 = bf16[512,1024]{1,0:T(8,128)(2,1)S(1)} copy-done((bf16[512,1024]{1,0:T(8,128)(2,1)S(1)}, bf16[512,1024]{1,0:T(8,128)(2,1)}, u32[]{:S(2)}) %copy-start.1) | copy-done | bytes 1048600
  3.3 0.0 copy-start.2
  3.3 0.7 copy-done.2
  4.0 0.0 copy-start.3
  4.0 0.7 copy-done.3
  4.7 80.1 %mix.1.got = bf16[8,36,16,128]{3,2,1,0:T(8,128)(2,1)S(1)} custom-call(bf16[512,1024]{1,0:T(8,128)(2,1)S(1)} %copy-done.1, bf16[512,3584]{1,0:T(8,128)(2,1)S(1)} %copy-done, s32[3584]{0:T(1024)S(1)} %copy-done.2, s32[4,8]{1,0:T(4,128)S(1)} %copy-done.3), custom_call_target="tpu_custom_call" | custom-call | tf_op jit(solution)/shard_map/mix/pallas_call | solution.py:551
  84.8 2.2 %assemble.1 = f32[1024,1024]{1,0:T(8,128)} custom-call(bf16[8,36,16,128]{3,2,1,0:T(8,128)(2,1)S(1)} %mix.1.got), custom_call_target="tpu_custom_call" | custom-call | tf_op jit(solution)/shard_map/assemble/pallas_call | solution.py:585
Async XLA Ops:
  0.0 2.0 %copy-start = (bf16[512,3584]{1,0:T(8,128)(2,1)S(1)}, bf16[512,3584]{1,0:T(8,128)(2,1)}, u32[]{:S(2)}) copy-start(bf16[512,3584]{1,0:T(8,128)(2,1)} %grads_hbm.1) | copy-start | bytes 11010052
  2.0 1.2 %copy-start.1 = (bf16[512,1024]{1,0:T(8,128)(2,1)S(1)}, bf16[512,1024]{1,0:T(8,128)(2,1)}, u32[]{:S(2)}) copy-start(bf16[512,1024]{1,0:T(8,128)(2,1)} %act_hbm.1) | copy-start | bytes 3145732
  3.3 0.7 copy-start.2
  4.0 0.7 copy-start.3

commit v2 on v1

--- a/solution.py
+++ b/solution.py
@@ -115,6 +115,7 @@
     inv_block = 1.0 / math.sqrt(width)
     inv_shard = 1.0 / math.sqrt(shards)
     quarter = width // CUTS
+    most = len(CHUNKS[1])
 
     barrier = pltpu.get_barrier_semaphore()
 
@@ -141,7 +142,7 @@
         pltpu.make_async_copy(ids_hbm, ids, l_sem.at[1]),
         pltpu.make_async_copy(bits_hbm, bits, l_sem.at[2]),
     ) + tuple(
-        pltpu.make_async_copy(grads_hbm.at[:, pl.ds(width * b, width)], grads.at[b], l_sem.at[3 + b]) for b in range(per)
+        pltpu.make_async_copy(grads_hbm.at[:, pl.ds(width * b, width)], grads.at[b], l_sem.at[3]) for b in range(per)
     )
     for load in loads:
         load.start()
@@ -188,7 +189,7 @@
         rows = pl.ds(quarter * h, quarter)
         n = GB + CUTS * k + h
         return pltpu.make_async_remote_copy(
-            tx.at[way, k, rows], rx.at[way, k, rows], z_send.at[way, n], z_recv.at[way, n],
+            tx.at[way, k, rows], rx.at[way, k, rows], z_send.at[way, 1], z_recv.at[way, n],
             device_id={"shard": who}, device_id_type=ALONG)
 
     def s_copy(way, k, h):
@@ -196,11 +197,19 @@
 
     def g_move(way, n, who):
         return pltpu.make_async_remote_copy(
-            gtx.at[way, n], grx.at[way, n], z_send.at[way, n], z_recv.at[way, n],
+            gtx.at[way, n], grx.at[way, n], z_send.at[way, 0], z_recv.at[way, n],
             device_id={"shard": who}, device_id_type=ALONG)
 
     def g_copy(way, n):
         return g_move(way, n, target(way))
+
+    def z_sent(way):
+        pltpu.make_async_remote_copy(
+            gtx.at[way], grx.at[way], z_send.at[way, 0], z_recv.at[way, 0],
+            device_id={"shard": target(way)}, device_id_type=ALONG).wait_send()
+        pltpu.make_async_remote_copy(
+            tx.at[way], rx.at[way], z_send.at[way, 1], z_recv.at[way, 0],
+            device_id={"shard": target(way)}, device_id_type=ALONG).wait_send()
 
     def gpart(n):
         i, j = TRIANGLE[n]
@@ -213,46 +222,58 @@
     def units(t, c):
         return pl.ds(*units_of(CHUNKS[t][c]))
 
-    def a_move(t, c, slot, who, holder):
+    def a_copy(t, c, slot, who):
+        arrival = a_recv.at[most] if slot == 3 else a_recv.at[c]
         return pltpu.make_async_remote_copy(
-            gathered.at[holder, units(t, c)], gathered.at[holder, units(t, c)], a_send.at[c, slot], a_recv.at[c, slot],
+            gathered.at[d, units(t, c)], gathered.at[d, units(t, c)], a_send.at[slot], arrival,
             device_id={"dp": who}, device_id_type=ALONG)
 
-    def w_move(t, c, m, holder):
+    def w_copy(t, c, m):
         return pltpu.make_async_remote_copy(
-            gathered.at[holder, units(t, c)], gathered.at[holder, units(t, c)],
-            w_send.at[c, m - 1], w_recv.at[c, m - 1],
+            gathered.at[peer(m), units(t, c)], gathered.at[peer(m), units(t, c)],
+            w_send.at[0], w_recv.at[0],
             device_id={"dp": partner}, device_id_type=ALONG)
 
     def spread(t, c):
         for m in (1, 2, 3):
-            a_move(t, c, m - 1, peer(m), d).start()
-        a_move(t, c, 3, partner, d).start()
+            a_copy(t, c, m - 1, peer(m)).start()
+        a_copy(t, c, 3, partner).start()
 
     def relay(t, c):
+        us = units(t, c)
+        pltpu.make_async_remote_copy(
+            gathered.at[0:3, us], gathered.at[0:3, us], a_send.at[0], a_recv.at[c],
+            device_id={"dp": partner}, device_id_type=ALONG).wait_recv()
         for m in (1, 2, 3):
-            a_move(t, c, m - 1, peer(m), peer(m)).wait_recv()
-            w_move(t, c, m, peer(m)).start()
-
-    def settle(t, c):
-        a_move(t, c, 3, partner, partner).wait_recv()
-        for m in (1, 2, 3):
-            w_move(t, c, m, peer(m) + 1 - 2 * core).wait_recv()
-        for m in (1, 2, 3):
-            a_move(t, c, m - 1, peer(m), d).wait_send()
-            w_move(t, c, m, peer(m)).wait_send()
-        a_move(t, c, 3, partner, d).wait_send()
+            w_copy(t, c, m).start()
+
+    def settle():
+        one = pltpu.make_async_remote_copy(
+            gathered.at[0], gathered.at[0], a_send.at[3], a_recv.at[most],
+            device_id={"dp": partner}, device_id_type=ALONG)
+        three = pltpu.make_async_remote_copy(
+            gathered.at[0:3], gathered.at[0:3], w_send.at[0], w_recv.at[0],
+            device_id={"dp": partner}, device_id_type=ALONG)
+        one.wait_recv()
+        three.wait_recv()
+        for slot in range(3):
+            pltpu.make_async_remote_copy(
+                gathered.at[0], gathered.at[0], a_send.at[slot], a_recv.at[0],
+                device_id={"dp": partner}, device_id_type=ALONG).wait_send()
+        one.wait_send()
+        three.wait_send()
 
     def f_copy(c, who):
         us = units(0, c)
         return pltpu.make_async_remote_copy(
-            rrx.at[3, us], gathered.at[d, us], f_send.at[c], f_recv.at[c],
+            rrx.at[3, us], gathered.at[d, us], f_send.at[0], f_recv.at[c],
             device_id={"shard": who}, device_id_type=ALONG)
 
     loads[0].wait()
     part[...] = lax.dot_general(act[...], act[...], (((1,), (1,)), ((), ())), preferred_element_type=jnp.float32)
-    for load in loads[1:]:
-        load.wait()
+    loads[1].wait()
+    loads[2].wait()
+    pltpu.make_async_copy(grads, grads, l_sem.at[3]).wait()
     for b in range(per):
         flips[b] = (1 - 2 * bits[width * b : width * (b + 1)].reshape(1, width)).astype(jnp.float32)
 
@@ -304,13 +325,13 @@
         def p_copy(q):
             t, c, k, us = where(q)
             return pltpu.make_async_remote_copy(
-                give.at[us], prx.at[us], p_send.at[q], p_recv.at[q],
+                give.at[us], prx.at[us], p_send.at[0], p_recv.at[q],
                 device_id={"dp": partner}, device_id_type=ALONG)
 
         def r_copy(q, m):
             t, c, k, us = where(q)
             return pltpu.make_async_remote_copy(
-                rtx.at[peer(m) // 2, us], rrx.at[m - 1, us], r_send.at[q, m - 1], r_recv.at[q, m - 1],
+                rtx.at[peer(m) // 2, us], rrx.at[m - 1, us], r_send.at[m - 1], r_recv.at[q],
                 device_id={"dp": peer(m)}, device_id_type=ALONG)
 
         def step_a(q):
@@ -356,8 +377,9 @@
 
         def step_c(q):
             t, c, k, us = where(q)
-            for m in (1, 2, 3):
-                r_copy(q, m).wait_recv()
+            pltpu.make_async_remote_copy(
+                rrx.at[0:3, us], rrx.at[0:3, us], r_send.at[0], r_recv.at[q],
+                device_id={"dp": partner}, device_id_type=ALONG).wait_recv()
             total = rtx[chip, us].astype(jnp.float32)
             for m in range(3):
                 total = total + rrx[m, us].astype(jnp.float32)
@@ -373,14 +395,20 @@
             t, c, k, us = where(q)
             if t == 1:
                 relay(t, c)
-            p_copy(q).wait_send()
-            for m in (1, 2, 3):
-                r_copy(q, m).wait_send()
-
-        def drain(k, carry):
-            for h in range(CUTS):
-                s_copy(out_way, k, h).wait_send()
-            return carry
+
+        def drain():
+            pltpu.make_async_remote_copy(
+                give, prx, p_send.at[0], p_recv.at[0],
+                device_id={"dp": partner}, device_id_type=ALONG).wait_send()
+            for m in range(3):
+                pltpu.make_async_remote_copy(
+                    rtx.at[m], rrx.at[m], r_send.at[m], r_recv.at[0],
+                    device_id={"dp": partner}, device_id_type=ALONG).wait_send()
+            us = pl.ds(0, UNITS)
+            pltpu.make_async_remote_copy(
+                rrx.at[3, us], gathered.at[d, us], f_send.at[0], f_recv.at[0],
+                device_id={"shard": side}, device_id_type=ALONG).wait_send()
+            z_sent(out_way)
 
         steps = len(STEPS)
         for q in range(steps - 3):
@@ -405,19 +433,12 @@
         step_c(e)
         step_c(e + 1)
         step_c(e + 2)
-        for n in range(GB):
-            g_copy(out_way, n).wait_send()
-        lax.fori_loop(0, PIECES, drain, 0)
-        for c in range(len(CHUNKS[1]) - 3):
-            settle(1, c)
         step_d(e - 1)
-        for c in range(len(CHUNKS[0])):
-            f_copy(c, side).wait_send()
         step_d(e)
         step_d(e + 1)
+        drain()
         step_d(e + 2)
-        for c in range(len(CHUNKS[1]) - 3, len(CHUNKS[1])):
-            settle(1, c)
+        settle()
 
     @pl.when(middle)
     def _():
@@ -470,34 +491,16 @@
             pass_s(far, PIECES - 1, h)
 
         chunks = len(CHUNKS[0])
-        for way in range(2):
-            for n in range(GB):
-                g_copy(way, n).wait_send()
-
-        def drain(k, carry):
-            for h in range(CUTS):
-                s_copy(near, k, h).wait_send()
-            return carry
-
-        def drain_far(k, carry):
-            for h in range(CUTS):
-                s_copy(far, k, h).wait_send()
-            return carry
-
-        lax.fori_loop(0, PIECES, drain, 0)
-        lax.fori_loop(0, PIECES - 2, drain_far, 0)
         for c in range(chunks):
             f_copy(c, outward).wait_recv()
             spread(0, c)
             if c >= 2:
                 relay(0, c - 2)
-        lax.fori_loop(PIECES - 2, PIECES, drain_far, 0)
+        z_sent(near)
+        z_sent(far)
         relay(0, chunks - 2)
-        for c in range(chunks - 2):
-            settle(0, c)
         relay(0, chunks - 1)
-        settle(0, chunks - 2)
-        settle(0, chunks - 1)
+        settle()
 
 
 def assemble_kernel(got, out, held, sems):
@@ -571,15 +574,15 @@
             pltpu.VMEM((2 * UNITS, 64, BLK), bf),
             pltpu.VMEM((4, 2 * UNITS, 16, BLK), bf),
             pltpu.VMEM((4, 2 * UNITS, 16, BLK), bf),
-            dma((3 + per,)),
-            dma((2, GB + CUTS * PIECES)), dma((2, GB + CUTS * PIECES)),
-            dma((steps,)), dma((steps,)),
-            dma((steps, 3)), dma((steps, 3)),
-            dma((COUNT,)), dma((COUNT,)),
-            dma((most, 4)), dma((most, 4)),
-            dma((most, 3)), dma((most, 3)),
+            dma((4,)),
+            dma((2, 2)), dma((2, GB + CUTS * PIECES)),
+            dma((1,)), dma((steps,)),
+            dma((3,)), dma((steps,)),
+            dma((1,)), dma((COUNT,)),
+            dma((4,)), dma((most + 1,)),
+            dma((1,)), dma((1,)),
         ],
-        compiler_params=pltpu.CompilerParams(collective_id=0, has_side_effects=True, vmem_limit_bytes=40 * 2**20),
+        compiler_params=pltpu.CompilerParams(collective_id=0, has_side_effects=True, vmem_limit_bytes=50 * 2**20),
         name="mix",
     )(activations, out_grads, sign_bits, block_ids)
     return pl.pallas_call(

time: 87.3 us -> 82.1 us (0.940)
  Pallas kernels: 82.4 us -> 79.2 us
  local copies, waits for them, and re-layouts: 4.66 us -> 2.62 us
    pallas_call x1, Pallas kernels: 80.1 us -> 77 us  [fast_body(): pl.pallas_call(functools.partial(mix_kernel, shards, parts, own, per), ou...]
    unnamed x8 -> x6, local copies, waits for them, and re-layouts: 4.66 us -> 2.62 us
where the time goes in v2:
time: 82.1 us; the launch traced here: 81.8 us
  Pallas kernels  79.2 us (96%)
  local copies, waits for them, and re-layouts  2.62 us (3%)
    pallas_call x1, Pallas kernels, fast_body(): pl.pallas_call(functools.partial(mix_kernel, shards, parts, own, per), ou...  77 us
    unnamed x6, local copies, waits for them, and re-layouts  2.62 us
    pallas_call x1, Pallas kernels, fast_body(): pl.pallas_call(assemble_kernel, out_shape=jax.ShapeDtypeStruct((own * BLK...  2.24 us

profile of v2, /device:TPU:0, one launch (start us, length us, event | category | flops | bytes accessed | tf_op | source)
XLA Modules:
  0.0 81.8 jit_solution(13852429013574004178)
XLA Ops:
  0.0 0.0 copy-start
  0.0 1.2 %copy-done = bf16[512,1024]{1,0:T(8,128)(2,1)S(1)} copy-done((bf16[512,1024]{1,0:T(8,128)(2,1)S(1)}, bf16[512,1024]{1,0:T(8,128)(2,1)}, u32[]{:S(2)}) %copy-start) | copy-done | bytes 1048600
  1.2 0.0 copy-start.1
  1.2 0.7 copy-done.1
  1.9 0.0 copy-start.2
  1.9 0.7 copy-done.2
  2.6 77.0 %mix.1.got = bf16[8,36,16,128]{3,2,1,0:T(8,128)(2,1)S(1)} custom-call(bf16[512,1024]{1,0:T(8,128)(2,1)S(1)} %copy-done, bf16[512,3584]{1,0:T(8,128)(2,1)} %grads_hbm.1, s32[3584]{0:T(1024)S(1)} %copy-done.1, s32[4,8]{1,0:T(4,128)S(1)} %copy-done.2), custom_call_target="tpu_custom_call" | custom-call | tf_op jit(solution)/shard_map/mix/pallas_call | solution.py:554
  79.6 2.2 %assemble.1 = f32[1024,1024]{1,0:T(8,128)} custom-call(bf16[8,36,16,128]{3,2,1,0:T(8,128)(2,1)S(1)} %mix.1.got), custom_call_target="tpu_custom_call" | custom-call | tf_op jit(solution)/shard_map/assemble/pallas_call | solution.py:588
Async XLA Ops:
  0.0 1.2 %copy-start = (bf16[512,1024]{1,0:T(8,128)(2,1)S(1)}, bf16[512,1024]{1,0:T(8,128)(2,1)}, u32[]{:S(2)}) copy-start(bf16[512,1024]{1,0:T(8,128)(2,1)} %act_hbm.1) | copy-start | bytes 3145732
  1.2 0.7 copy-start.1
  1.9 0.7 copy-start.2

commit v3 on v2

--- a/solution.py
+++ b/solution.py
@@ -79,8 +79,9 @@
 COUNT = 8
 PIECES = 2 * COUNT
 CUTS = 4
-GB = 10
-TRIANGLE = tuple((i, j) for i in range(4) for j in range(i + 1))
+GB = 9
+BELOW = tuple((i, j) for i in range(4) for j in range(i))
+ROWS = tuple(128 if n < GB - 1 else 16 for n in range(GB))
 UNITS = COUNT * (COUNT + 1) // 2
 ORDER = tuple((1, COUNT - 1) if k == PIECES - 1 else (0, (k + 1) // 2) if k % 2 or k == 0 else (1, k // 2 - 1) for k in range(PIECES))
 WHOLE = tuple((j, 0, BLK) for j in range(COUNT))
@@ -100,7 +101,7 @@
 
 def mix_kernel(
     shards, parts, own, per, act_hbm, grads_hbm, bits_hbm, ids_hbm, gathered,
-    act, grads, bits, flips, ids, rx, tx, grx, gtx, part, full, sketch, keep, give, prx, rtx, rrx,
+    act, grads, bits, flips, ids, rx, tx, grx, gtx, part, pairs, diagonals, full, sketch, keep, give, prx, rtx, rrx,
     l_sem, z_send, z_recv, p_send, p_recv, r_send, r_recv, f_send, f_recv, a_send, a_recv, w_send, w_recv,
 ):
     z = lax.axis_index("shard")
@@ -196,8 +197,9 @@
         return s_move(way, k, h, target(way))
 
     def g_move(way, n, who):
+        rows = pl.ds(0, ROWS[n])
         return pltpu.make_async_remote_copy(
-            gtx.at[way, n], grx.at[way, n], z_send.at[way, 0], z_recv.at[way, n],
+            gtx.at[way, n, rows], grx.at[way, n, rows], z_send.at[way, 2 * (n // (GB - 1))], z_recv.at[way, n],
             device_id={"shard": who}, device_id_type=ALONG)
 
     def g_copy(way, n):
@@ -205,15 +207,25 @@
 
     def z_sent(way):
         pltpu.make_async_remote_copy(
-            gtx.at[way], grx.at[way], z_send.at[way, 0], z_recv.at[way, 0],
+            gtx.at[way, 0 : GB - 1], grx.at[way, 0 : GB - 1], z_send.at[way, 0], z_recv.at[way, 0],
             device_id={"shard": target(way)}, device_id_type=ALONG).wait_send()
+        g_copy(way, GB - 1).wait_send()
         pltpu.make_async_remote_copy(
             tx.at[way], rx.at[way], z_send.at[way, 1], z_recv.at[way, 0],
             device_id={"shard": target(way)}, device_id_type=ALONG).wait_send()
 
+    def square(i, j):
+        return part[128 * i : 128 * (i + 1), 128 * j : 128 * (j + 1)]
+
     def gpart(n):
-        i, j = TRIANGLE[n]
-        return part[128 * i : 128 * (i + 1), 128 * j : 128 * (j + 1)]
+        if n < len(BELOW):
+            return square(*BELOW[n])
+        if n < GB - 1:
+            return pairs[n - len(BELOW)]
+        return diagonals[...]
+
+    def gsum(way, n):
+        return (grx[way, n, : ROWS[n]].astype(jnp.float32) + gpart(n)).astype(jnp.bfloat16)
 
     def fill(way, k):
         t, j = piece(k)
@@ -271,6 +283,11 @@
 
     loads[0].wait()
     part[...] = lax.dot_general(act[...], act[...], (((1,), (1,)), ((), ())), preferred_element_type=jnp.float32)
+    diagonals[...] = jnp.zeros_like(diagonals)
+    for n in range(2):
+        second = square(2 * n + 1, 2 * n + 1)
+        pairs[n] = jnp.where(row >= col, square(2 * n, 2 * n), second)
+        diagonals[n : n + 1] = jnp.sum(jnp.where(row == col, second, 0.0), axis=0, keepdims=True)
     loads[1].wait()
     loads[2].wait()
     pltpu.make_async_copy(grads, grads, l_sem.at[3]).wait()
@@ -291,7 +308,7 @@
         in_way = 1 - out_way
         side = target(out_way)
         for n in range(GB):
-            gtx[out_way, n] = gpart(n).astype(jnp.bfloat16)
+            gtx[out_way, n, : ROWS[n]] = gpart(n).astype(jnp.bfloat16)
             g_copy(out_way, n).start()
 
         def push(k, carry):
@@ -311,11 +328,19 @@
 
         for n in range(GB):
             g_move(in_way, n, side).wait_recv()
-            r, c = TRIANGLE[n]
-            block = (grx[in_way, n].astype(jnp.float32) + gpart(n)).astype(jnp.bfloat16)
-            full[128 * r : 128 * (r + 1), 128 * c : 128 * (c + 1)] = block
-            if r != c:
+            if n < len(BELOW):
+                r, c = BELOW[n]
+                block = gsum(in_way, n)
+                full[128 * r : 128 * (r + 1), 128 * c : 128 * (c + 1)] = block
                 full[128 * c : 128 * (c + 1), 128 * r : 128 * (r + 1)] = block.T
+        ends = gsum(in_way, GB - 1).astype(jnp.float32)
+        for n in range(2):
+            both_of = gsum(in_way, len(BELOW) + n).astype(jnp.float32)
+            turned = both_of.T
+            first = jnp.where(row >= col, both_of, turned)
+            second = jnp.where(row < col, both_of, jnp.where(row > col, turned, ends[n : n + 1]))
+            for i, block in ((2 * n, first), (2 * n + 1, second)):
+                full[128 * i : 128 * (i + 1), 128 * i : 128 * (i + 1)] = block.astype(jnp.bfloat16)
 
         def where(q):
             t, c, k = STEPS[q]
@@ -448,7 +473,7 @@
 
         def pass_g(way, n):
             g_copy(way, n).wait_recv()
-            gtx[way, n] = (grx[way, n].astype(jnp.float32) + gpart(n)).astype(jnp.bfloat16)
+            gtx[way, n, : ROWS[n]] = gsum(way, n)
             g_copy(way, n).start()
 
         def pass_s(way, k, h):
@@ -567,6 +592,8 @@
             pltpu.VMEM((2, GB, 128, 128), bf),
             pltpu.VMEM((2, GB, 128, 128), bf),
             pltpu.VMEM((tokens, tokens), f32),
+            pltpu.VMEM((2, 128, 128), f32),
+            pltpu.VMEM((16, 128), f32),
             pltpu.VMEM((tokens, tokens), bf),
             pltpu.VMEM((2, own * BLK, tokens), bf),
             pltpu.VMEM((2 * UNITS, 64, BLK), f32),
@@ -575,7 +602,7 @@
             pltpu.VMEM((4, 2 * UNITS, 16, BLK), bf),
             pltpu.VMEM((4, 2 * UNITS, 16, BLK), bf),
             dma((4,)),
-            dma((2, 2)), dma((2, GB + CUTS * PIECES)),
+            dma((2, 3)), dma((2, GB + CUTS * PIECES)),
             dma((1,)), dma((steps,)),
             dma((3,)), dma((steps,)),
             dma((1,)), dma((COUNT,)),

time: 82.1 us -> 80.9 us (0.985)
  Pallas kernels: 79.2 us -> 78 us
    pallas_call x1, Pallas kernels: 77 us -> 75.8 us  [fast_body(): pl.pallas_call(functools.partial(mix_kernel, shards, parts, own, per), ou...]
where the time goes in v3:
time: 80.9 us; the launch traced here: 80.7 us
  Pallas kernels  78 us (96%)
  local copies, waits for them, and re-layouts  2.62 us (3%)
    pallas_call x1, Pallas kernels, fast_body(): pl.pallas_call(functools.partial(mix_kernel, shards, parts, own, per), ou...  75.8 us
    unnamed x6, local copies, waits for them, and re-layouts  2.62 us
    pallas_call x1, Pallas kernels, fast_body(): pl.pallas_call(assemble_kernel, out_shape=jax.ShapeDtypeStruct((own * BLK...  2.24 us

profile of v3, /device:TPU:0, one launch (start us, length us, event | category | flops | bytes accessed | tf_op | source)
XLA Modules:
  0.0 80.7 jit_solution(12236951408360238513)
XLA Ops:
  0.0 0.0 copy-start
  0.0 1.2 %copy-done = bf16[512,1024]{1,0:T(8,128)(2,1)S(1)} copy-done((bf16[512,1024]{1,0:T(8,128)(2,1)S(1)}, bf16[512,1024]{1,0:T(8,128)(2,1)}, u32[]{:S(2)}) %copy-start) | copy-done | bytes 1048600
  1.2 0.0 copy-start.1
  1.2 0.7 copy-done.1
  1.9 0.0 copy-start.2
  1.9 0.7 copy-done.2
  2.6 75.8 %mix.1.got = bf16[8,36,16,128]{3,2,1,0:T(8,128)(2,1)S(1)} custom-call(bf16[512,1024]{1,0:T(8,128)(2,1)S(1)} %copy-done, bf16[512,3584]{1,0:T(8,128)(2,1)} %grads_hbm.1, s32[3584]{0:T(1024)S(1)} %copy-done.1, s32[4,8]{1,0:T(4,128)S(1)} %copy-done.2), custom_call_target="tpu_custom_call" | custom-call | tf_op jit(solution)/shard_map/mix/pallas_call | solution.py:579
  78.4 2.2 %assemble.1 = f32[1024,1024]{1,0:T(8,128)} custom-call(bf16[8,36,16,128]{3,2,1,0:T(8,128)(2,1)S(1)} %mix.1.got), custom_call_target="tpu_custom_call" | custom-call | tf_op jit(solution)/shard_map/assemble/pallas_call | solution.py:615
Async XLA Ops:
  0.0 1.2 %copy-start = (bf16[512,1024]{1,0:T(8,128)(2,1)S(1)}, bf16[512,1024]{1,0:T(8,128)(2,1)}, u32[]{:S(2)}) copy-start(bf16[512,1024]{1,0:T(8,128)(2,1)} %act_hbm.1) | copy-start | bytes 3145732
  1.2 0.7 copy-start.1
  1.9 0.7 copy-start.2

commit v4 on v3

--- a/solution.py
+++ b/solution.py
@@ -100,9 +100,9 @@
 
 
 def mix_kernel(
-    shards, parts, own, per, act_hbm, grads_hbm, bits_hbm, ids_hbm, gathered,
-    act, grads, bits, flips, ids, rx, tx, grx, gtx, part, pairs, diagonals, full, sketch, keep, give, prx, rtx, rrx,
-    l_sem, z_send, z_recv, p_send, p_recv, r_send, r_recv, f_send, f_recv, a_send, a_recv, w_send, w_recv,
+    shards, parts, own, per, act_hbm, grads_hbm, bits_hbm, ids_hbm, got,
+    act, grads, bits, flips, ids, rx, tx, grx, gtx, part, pairs, diagonals, full, sketch, keep, give, prx, rtx, rrx, gathered,
+    l_sem, o_sem, z_send, z_recv, p_send, p_recv, r_send, r_recv, f_send, f_recv, a_send, a_recv, w_send, w_recv,
 ):
     z = lax.axis_index("shard")
     d = lax.axis_index("dp")
@@ -234,8 +234,11 @@
     def units(t, c):
         return pl.ds(*units_of(CHUNKS[t][c]))
 
+    def late(t, c):
+        return int(CHUNKS[t][c][0] >= COUNT - 2)
+
     def a_copy(t, c, slot, who):
-        arrival = a_recv.at[most] if slot == 3 else a_recv.at[c]
+        arrival = a_recv.at[most + late(t, c)] if slot == 3 else a_recv.at[c]
         return pltpu.make_async_remote_copy(
             gathered.at[d, units(t, c)], gathered.at[d, units(t, c)], a_send.at[slot], arrival,
             device_id={"dp": who}, device_id_type=ALONG)
@@ -243,7 +246,7 @@
     def w_copy(t, c, m):
         return pltpu.make_async_remote_copy(
             gathered.at[peer(m), units(t, c)], gathered.at[peer(m), units(t, c)],
-            w_send.at[0], w_recv.at[0],
+            w_send.at[0], w_recv.at[late(t, c)],
             device_id={"dp": partner}, device_id_type=ALONG)
 
     def spread(t, c):
@@ -259,21 +262,33 @@
         for m in (1, 2, 3):
             w_copy(t, c, m).start()
 
-    def settle():
-        one = pltpu.make_async_remote_copy(
-            gathered.at[0], gathered.at[0], a_send.at[3], a_recv.at[most],
-            device_id={"dp": partner}, device_id_type=ALONG)
-        three = pltpu.make_async_remote_copy(
-            gathered.at[0:3], gathered.at[0:3], w_send.at[0], w_recv.at[0],
-            device_id={"dp": partner}, device_id_type=ALONG)
-        one.wait_recv()
-        three.wait_recv()
-        for slot in range(3):
+    early = (COUNT - 2) * (COUNT - 1) // 2
+    GROUPS = ((0, early), (early, UNITS))
+
+    def leave(g):
+        us = pl.ds(GROUPS[g][0], GROUPS[g][1] - GROUPS[g][0])
+        return pltpu.make_async_copy(gathered.at[:, us], got.at[:, us], o_sem.at[g])
+
+    def settle(g):
+        us = pl.ds(GROUPS[g][0], GROUPS[g][1] - GROUPS[g][0])
+        pltpu.make_async_remote_copy(
+            gathered.at[0, us], gathered.at[0, us], a_send.at[3], a_recv.at[most + g],
+            device_id={"dp": partner}, device_id_type=ALONG).wait_recv()
+        pltpu.make_async_remote_copy(
+            gathered.at[0:3, us], gathered.at[0:3, us], w_send.at[0], w_recv.at[g],
+            device_id={"dp": partner}, device_id_type=ALONG).wait_recv()
+        leave(g).start()
+
+    def finish():
+        for slot in range(4):
             pltpu.make_async_remote_copy(
                 gathered.at[0], gathered.at[0], a_send.at[slot], a_recv.at[0],
                 device_id={"dp": partner}, device_id_type=ALONG).wait_send()
-        one.wait_send()
-        three.wait_send()
+        pltpu.make_async_remote_copy(
+            gathered.at[0:3], gathered.at[0:3], w_send.at[0], w_recv.at[0],
+            device_id={"dp": partner}, device_id_type=ALONG).wait_send()
+        for g in range(2):
+            leave(g).wait()
 
     def f_copy(c, who):
         us = units(0, c)
@@ -288,11 +303,12 @@
         second = square(2 * n + 1, 2 * n + 1)
         pairs[n] = jnp.where(row >= col, square(2 * n, 2 * n), second)
         diagonals[n : n + 1] = jnp.sum(jnp.where(row == col, second, 0.0), axis=0, keepdims=True)
-    loads[1].wait()
-    loads[2].wait()
-    pltpu.make_async_copy(grads, grads, l_sem.at[3]).wait()
-    for b in range(per):
-        flips[b] = (1 - 2 * bits[width * b : width * (b + 1)].reshape(1, width)).astype(jnp.float32)
+    def loaded():
+        loads[1].wait()
+        loads[2].wait()
+        pltpu.make_async_copy(grads, grads, l_sem.at[3]).wait()
+        for b in range(per):
+            flips[b] = (1 - 2 * bits[width * b : width * (b + 1)].reshape(1, width)).astype(jnp.float32)
 
     @pl.when(edge)
     def _():
@@ -310,6 +326,7 @@
         for n in range(GB):
             gtx[out_way, n, : ROWS[n]] = gpart(n).astype(jnp.bfloat16)
             g_copy(out_way, n).start()
+        loaded()
 
         def push(k, carry):
             fill(out_way, k)
@@ -359,10 +376,12 @@
                 rtx.at[peer(m) // 2, us], rrx.at[m - 1, us], r_send.at[m - 1], r_recv.at[q],
                 device_id={"dp": peer(m)}, device_id_type=ALONG)
 
-        def step_a(q):
+        def step_a(q, between=None):
             t, c, k, us = where(q)
             j, lo, hi = CHUNKS[t][c]
             for h in range(lo // quarter, hi // quarter):
+                if between is not None and h == CUTS - 1:
+                    step_c(between)
                 s_move(in_way, k, h, side).wait_recv()
                 rows = slice(width * j + quarter * h, width * j + quarter * (h + 1))
                 arrived = rx[in_way, k, quarter * h : quarter * (h + 1)].astype(jnp.float32)
@@ -437,15 +456,12 @@
 
         steps = len(STEPS)
         for q in range(steps - 3):
-            step_a(q)
+            step_a(q, q - 2 if q >= 2 else None)
             step_b(q)
-            if q >= 2:
-                step_c(q - 2)
             if q >= 4:
                 step_d(q - 4)
         e = steps - 3
-        step_a(e)
-        step_c(e - 2)
+        step_a(e, e - 2)
         step_a(e + 1)
         step_b(e)
         step_a(e + 2)
@@ -462,14 +478,17 @@
         step_d(e)
         step_d(e + 1)
         drain()
+        settle(0)
         step_d(e + 2)
-        settle()
+        settle(1)
+        finish()
 
     @pl.when(middle)
     def _():
         near = jnp.where(z == 1, 1, 0)
         far = 1 - near
         outward = jnp.where(z == 1, 0, last)
+        loaded()
 
         def pass_g(way, n):
             g_copy(way, n).wait_recv()
@@ -524,11 +543,16 @@
         z_sent(near)
         z_sent(far)
         relay(0, chunks - 2)
+        settle(0)
         relay(0, chunks - 1)
-        settle()
-
-
-def assemble_kernel(got, out, held, sems):
+        settle(1)
+        finish()
+
+
+def assemble_kernel(source, out, got, held, sems):
+    load = pltpu.make_async_copy(source, got, sems.at[COUNT])
+    load.start()
+    load.wait()
     half = BLK // 2
 
     def unit(u):
@@ -571,7 +595,6 @@
     tokens, columns = out_grads.shape
     per = columns // BLK
     own = block_ids.shape[1]
-    vmem = pl.BlockSpec(memory_space=pltpu.VMEM)
     hbm = pl.BlockSpec(memory_space=pltpu.HBM)
     bf, f32 = jnp.bfloat16, jnp.float32
     dma = pltpu.SemaphoreType.DMA
@@ -580,7 +603,7 @@
         functools.partial(mix_kernel, shards, parts, own, per),
         out_shape=jax.ShapeDtypeStruct((parts, UNITS, 16, BLK), bf),
         in_specs=[hbm, hbm, hbm, hbm],
-        out_specs=vmem,
+        out_specs=hbm,
         scratch_shapes=[
             pltpu.VMEM(activations.shape, bf),
             pltpu.VMEM((per, tokens, BLK), bf),
@@ -601,24 +624,26 @@
             pltpu.VMEM((2 * UNITS, 64, BLK), bf),
             pltpu.VMEM((4, 2 * UNITS, 16, BLK), bf),
             pltpu.VMEM((4, 2 * UNITS, 16, BLK), bf),
-            dma((4,)),
+            pltpu.VMEM((parts, UNITS, 16, BLK), bf),
+            dma((4,)), dma((2,)),
             dma((2, 3)), dma((2, GB + CUTS * PIECES)),
             dma((1,)), dma((steps,)),
             dma((3,)), dma((steps,)),
             dma((1,)), dma((COUNT,)),
-            dma((4,)), dma((most + 1,)),
-            dma((1,)), dma((1,)),
+            dma((4,)), dma((most + 2,)),
+            dma((1,)), dma((2,)),
         ],
-        compiler_params=pltpu.CompilerParams(collective_id=0, has_side_effects=True, vmem_limit_bytes=50 * 2**20),
+        compiler_params=pltpu.CompilerParams(collective_id=0, has_side_effects=True, vmem_limit_bytes=int(62.5 * 2**20)),
         name="mix",
     )(activations, out_grads, sign_bits, block_ids)
     return pl.pallas_call(
         assemble_kernel,
         out_shape=jax.ShapeDtypeStruct((own * BLK, own * BLK), f32),
-        in_specs=[vmem],
+        in_specs=[hbm],
         out_specs=hbm,
-        scratch_shapes=[pltpu.VMEM((own * BLK, own * BLK), f32), dma((own,))],
-        compiler_params=pltpu.CompilerParams(vmem_limit_bytes=16 * 2**20),
+        scratch_shapes=[
+            pltpu.VMEM((parts, UNITS, 16, BLK), bf), pltpu.VMEM((own * BLK, own * BLK), f32), dma((own + 1,))],
+        compiler_params=pltpu.CompilerParams(vmem_limit_bytes=int(62.5 * 2**20)),
         name="assemble",
     )(got)
 

time: 80.9 us -> 79.8 us (0.986)
  local copies, waits for them, and re-layouts: 2.62 us -> 0 us
  Pallas kernels: 78 us -> 79.3 us
    unnamed x6 -> x0, local copies, waits for them, and re-layouts: 2.62 us -> none
    pallas_call x1, Pallas kernels: 2.24 us -> 3.52 us  [fast_body(): pl.pallas_call(assemble_kernel, out_shape=jax.ShapeDtypeStruct((own * BLK...]
where the time goes in v4:
time: 79.8 us; the launch traced here: 79.4 us
  Pallas kernels  79.3 us (99%)
    pallas_call x1, Pallas kernels, fast_body(): pl.pallas_call(functools.partial(mix_kernel, shards, parts, own, per), ou...  75.8 us
    pallas_call x1, Pallas kernels, fast_body(): pl.pallas_call(assemble_kernel, out_shape=jax.ShapeDtypeStruct((own * BLK...  3.52 us

profile of v4, /device:TPU:0, one launch (start us, length us, event | category | flops | bytes accessed | tf_op | source)
XLA Modules:
  0.0 79.4 jit_solution(9978786129872747202)
XLA Ops:
  0.0 75.8 %mix.1.source = bf16[8,36,16,128]{3,2,1,0:T(8,128)(2,1)} custom-call(bf16[512,1024]{1,0:T(8,128)(2,1)} %act_hbm.1, bf16[512,3584]{1,0:T(8,128)(2,1)} %grads_hbm.1, s32[3584]{0:T(1024)} %bits_hbm.1, s32[4,8]{1,0:T(4,128)} %ids_hbm.1), custom_call_target="tpu_custom_call" | custom-call | tf_op jit(solution)/shard_map/mix/pallas_call | solution.py:602
  75.8 3.5 %assemble.1 = f32[1024,1024]{1,0:T(8,128)} custom-call(bf16[8,36,16,128]{3,2,1,0:T(8,128)(2,1)} %mix.1.source), custom_call_target="tpu_custom_call" | custom-call | tf_op jit(solution)/shard_map/assemble/pallas_call | solution.py:639

commit v5 on v4

--- a/solution.py
+++ b/solution.py
@@ -550,9 +550,12 @@
 
 
 def assemble_kernel(source, out, got, held, sems):
-    load = pltpu.make_async_copy(source, got, sems.at[COUNT])
-    load.start()
-    load.wait()
+    loads = []
+    for i in range(COUNT):
+        us = pl.ds(i * (i + 1) // 2, i + 1)
+        loads.append(pltpu.make_async_copy(source.at[:, us], got.at[:, us], sems.at[COUNT + i]))
+    for load in reversed(loads):
+        load.start()
     half = BLK // 2
 
     def unit(u):
@@ -566,6 +569,7 @@
     final = COUNT - 1
     first = final * COUNT // 2
     lower = {}
+    loads[final].wait()
     for v in range(COUNT // 2):
         top, bottom = unit(first + v), unit(first + COUNT // 2 + v)
         for g in range(2):
@@ -575,7 +579,9 @@
     row = lax.broadcasted_iota(jnp.int32, (BLK, BLK), 0)
     col = lax.broadcasted_iota(jnp.int32, (BLK, BLK), 1)
     lower[final] = jnp.where((row < half) & (col >= half), square.T, square)
-    for i in range(COUNT):
+    for i in reversed(range(COUNT)):
+        if i < final:
+            loads[i].wait()
         for j in range(COUNT):
             if i == final:
                 block = lower[j]
@@ -642,7 +648,7 @@
         in_specs=[hbm],
         out_specs=hbm,
         scratch_shapes=[
-            pltpu.VMEM((parts, UNITS, 16, BLK), bf), pltpu.VMEM((own * BLK, own * BLK), f32), dma((own + 1,))],
+            pltpu.VMEM((parts, UNITS, 16, BLK), bf), pltpu.VMEM((own * BLK, own * BLK), f32), dma((2 * own,))],
         compiler_params=pltpu.CompilerParams(vmem_limit_bytes=int(62.5 * 2**20)),
         name="assemble",
     )(got)

time: 79.8 us -> 79.5 us (level)
  no operation moved by 1% of the time
where the time goes in v5:
time: 79.5 us; the launch traced here: 79 us
  Pallas kernels  79 us (99%)
    pallas_call x1, Pallas kernels, fast_body(): pl.pallas_call(functools.partial(mix_kernel, shards, parts, own, per), ou...  75.8 us
    pallas_call x1, Pallas kernels, fast_body(): pl.pallas_call(assemble_kernel, out_shape=jax.ShapeDtypeStruct((own * BLK...  3.19 us

profile of v5, /device:TPU:0, one launch (start us, length us, event | category | flops | bytes accessed | tf_op | source)
XLA Modules:
  0.0 79.0 jit_solution(1576632990792416821)
XLA Ops:
  0.0 75.8 %mix.1.source = bf16[8,36,16,128]{3,2,1,0:T(8,128)(2,1)} custom-call(bf16[512,1024]{1,0:T(8,128)(2,1)} %act_hbm.1, bf16[512,3584]{1,0:T(8,128)(2,1)} %grads_hbm.1, s32[3584]{0:T(1024)} %bits_hbm.1, s32[4,8]{1,0:T(4,128)} %ids_hbm.1), custom_call_target="tpu_custom_call" | custom-call | tf_op jit(solution)/shard_map/mix/pallas_call | solution.py:608
  75.8 3.2 %assemble.1 = f32[1024,1024]{1,0:T(8,128)} custom-call(bf16[8,36,16,128]{3,2,1,0:T(8,128)(2,1)} %mix.1.source), custom_call_target="tpu_custom_call" | custom-call | tf_op jit(solution)/shard_map/assemble/pallas_call | solution.py:645
